TPU v7x, 512 devices: a whole 4x4x16 slice. The times are simulated.
512 devices in a mesh: dp: 32 (over x, y, core), expert: 16 (over z).
Axes of the slice: x: 4, y: 4, z: 16, core: 2. Of those that a mesh axis runs over, the one named last changes fastest.
Arguments:
- tokens: bfloat16 [4096, 2048], P('dp', 'expert'), may hold values from -6 to 6
- cotangent: bfloat16 [4096, 2048], P('dp', 'expert'), may hold values from -6 to 6
- expert_ids: int32 [4096, 8], P('dp'), may hold values from 0 to 127, all different within a row; in each aligned block of 128 rows (0 to 127, 128 to 255, ...) at most 16 rows name the same one
- gate_weights: float32 [4096, 8], P('dp'), may hold values from 0.05 to 1
- w_gate: bfloat16 [512, 192, 2048], P(('dp', 'expert')), may hold values from -0.125 to 0.125
- w_up: bfloat16 [512, 192, 2048], P(('dp', 'expert')), may hold values from -0.125 to 0.125
- w_down: bfloat16 [512, 192, 2048], P(('dp', 'expert')), may hold values from -0.21875 to 0.21875
Outputs:
- layer_out: bfloat16 [4096, 2048], P('dp', 'expert')
- grad_tokens: bfloat16 [4096, 2048], P('dp', 'expert')
- grad_gates: float32 [4096, 8], P('dp')
- grad_w_gate: bfloat16 [512, 192, 2048], P(('dp', 'expert'))
- grad_w_up: bfloat16 [512, 192, 2048], P(('dp', 'expert'))
- grad_w_down: bfloat16 [512, 192, 2048], P(('dp', 'expert'))
Inputs may be any that keep to these rules, and one draw needn't show every extreme that they name: `expert_ids`: each row names 8 different experts. In each aligned block of 128 rows (the rows of one index of dp) no expert is named by more than 16 rows, and in some block an expert is named by exactly 16 rows.
All inputs are finite; a program needn't handle non-finite values.
Results may differ from a plain program's by a relative error of at most 0.0064.
Values may be sent and summed in bfloat16 or wider, within the bound.
No kernel may reach another device: no remote copies, remote signals or barrier semaphores. Data moves between devices by JAX's collectives and lax.ppermute only.
A program may use at most 64 MiB of HBM per device.

v0:
```python
import jax
import jax.numpy as jnp
from jax import lax
from jax.sharding import PartitionSpec as P

SHARDS = 4


def silu_parts(preact):
    sigmoid_of = jax.nn.sigmoid(preact)
    activated = preact * sigmoid_of
    derivative = sigmoid_of * (1.0 + preact * (1.0 - sigmoid_of))
    return (activated, derivative)


def contract_last(first_op, second_op):
    return lax.dot_general(
        first_op, second_op, (((1,), (1,)), ((), ())), preferred_element_type=jnp.float32
    )


def contract_first(first_op, second_op):
    return lax.dot_general(
        first_op, second_op, (((0,), (0,)), ((), ())), preferred_element_type=jnp.float32
    )


def expert_rows(rows_x, rows_do, gate_w, up_w, down_w):
    pre_gate = contract_last(rows_x, gate_w)
    pre_up = contract_last(rows_x, up_w)
    activated, derivative = silu_parts(pre_gate)
    hidden = (activated * pre_up).astype(jnp.bfloat16)
    part_out = jnp.dot(hidden, down_w, preferred_element_type=jnp.float32).astype(jnp.bfloat16)
    d_hidden = contract_last(rows_do, down_w)
    d_pre_gate = (d_hidden * pre_up * derivative).astype(jnp.bfloat16)
    d_pre_up = (d_hidden * activated).astype(jnp.bfloat16)
    part_grad = (
        jnp.dot(d_pre_gate, gate_w, preferred_element_type=jnp.float32)
        + jnp.dot(d_pre_up, up_w, preferred_element_type=jnp.float32)
    ).astype(jnp.bfloat16)
    gradients = (
        contract_first(d_pre_gate, rows_x),
        contract_first(d_pre_up, rows_x),
        contract_first(hidden, rows_do),
    )
    return (part_out, part_grad, gradients)


def per_device(tokens, cotangent, expert_ids, gate_weights, w_gate, w_up, w_down):
    both = lax.all_gather(jnp.stack([tokens, cotangent]), "expert", axis=2, tiled=True)
    full_x, full_dy = (both[0], both[1])
    dp_count = lax.axis_size("dp")
    column_count = lax.axis_size("expert")
    column = lax.axis_index("expert")
    tok_count, chosen = expert_ids.shape
    features = full_x.shape[1]
    experts_all = dp_count * column_count // SHARDS
    capacity = min(tok_count, max(2, 2 * tok_count * chosen // experts_all))
    per_row = column_count // SHARDS
    assigned = tok_count * chosen
    flat_ids = expert_ids.reshape(-1)
    flat_gates = gate_weights.reshape(-1)
    owned_here = flat_ids % per_row == column // SHARDS
    target_row = flat_ids // per_row
    onehot = (
        (target_row[:, None] == jnp.arange(dp_count, dtype=jnp.int32)[None, :])
        & owned_here[:, None]
    ).astype(jnp.int32)
    rank_of = jnp.sum((jnp.cumsum(onehot, axis=0) - 1) * onehot, axis=1)
    target = jnp.where(owned_here, target_row * capacity + rank_of, dp_count * capacity)
    slot_src = (
        jnp.full((dp_count * capacity,), assigned, jnp.int32)
        .at[target]
        .set(jnp.arange(assigned, dtype=jnp.int32), mode="drop")
    )
    filled = slot_src < assigned
    safe_index = jnp.where(filled, slot_src, 0)
    slot_token = safe_index // chosen
    slot_gate = jnp.where(filled, flat_gates[safe_index], 0.0)
    slot_dy = full_dy[slot_token].astype(jnp.float32)
    send_x = jnp.where(filled[:, None], full_x[slot_token], jnp.zeros((), full_x.dtype)).reshape(
        dp_count, capacity, features
    )
    send_do = (
        (slot_gate[:, None] * slot_dy).astype(jnp.bfloat16).reshape(dp_count, capacity, features)
    )
    weights = (w_gate[0], w_up[0], w_down[0])
    recv = lax.all_to_all(
        jnp.concatenate([send_x, send_do], axis=1), "dp", split_axis=0, concat_axis=0, tiled=True
    )
    rows_x = recv[:, :capacity].reshape(dp_count * capacity, features)
    rows_do = recv[:, capacity:].reshape(dp_count * capacity, features)
    part_out, part_grad, gradients = expert_rows(rows_x, rows_do, *weights)
    back = lax.all_to_all(
        jnp.concatenate(
            [
                part_out.reshape(dp_count, capacity, features),
                part_grad.reshape(dp_count, capacity, features),
            ],
            axis=1,
        ),
        "dp",
        split_axis=0,
        concat_axis=0,
        tiled=True,
    )
    out_float = back[:, :capacity].reshape(dp_count * capacity, features).astype(jnp.float32)
    grad_float = back[:, capacity:].reshape(dp_count * capacity, features).astype(jnp.float32)
    out_part = (
        jnp.zeros((tok_count, features), jnp.float32)
        .at[slot_token]
        .add(slot_gate[:, None] * out_float)
    )
    grad_part = jnp.zeros((tok_count, features), jnp.float32).at[slot_token].add(grad_float)
    gate_terms = jnp.sum(slot_dy * out_float, axis=1)
    gate_part = (
        jnp.zeros((assigned,), jnp.float32)
        .at[slot_src]
        .add(gate_terms, mode="drop")
        .reshape(tok_count, chosen)
    )
    summed = lax.psum_scatter(
        jnp.stack([out_part, grad_part]), "expert", scatter_dimension=2, tiled=True
    )
    grad_gates = lax.psum(gate_part, "expert")
    return (
        summed[0].astype(jnp.bfloat16),
        summed[1].astype(jnp.bfloat16),
        grad_gates,
        gradients[0].astype(jnp.bfloat16)[None],
        gradients[1].astype(jnp.bfloat16)[None],
        gradients[2].astype(jnp.bfloat16)[None],
    )


def solution(mesh):
    placed = (
        P("dp", "expert"),
        P("dp", "expert"),
        P("dp", None),
        P("dp", None),
        P(("dp", "expert"), None, None),
        P(("dp", "expert"), None, None),
        P(("dp", "expert"), None, None),
    )
    return jax.shard_map(
        per_device,
        mesh=mesh,
        in_specs=placed,
        out_specs=(
            P("dp", "expert"),
            P("dp", "expert"),
            P("dp", None),
            P(("dp", "expert"), None, None),
            P(("dp", "expert"), None, None),
            P(("dp", "expert"), None, None),
        ),
        check_vma=False,
    )
```

profile of v0, /device:TPU:2, one launch (start us, length us, event | category | flops | bytes accessed | tf_op | source)
XLA Modules:
  0.0 319.4 jit_solution(1115190527233137053)
XLA Ops:
  7.2 1.5 pad_maximum_fusion.3
  8.8 0.8 copy.13
  9.9 0.8 copy.18
  10.8 9.0 %reduce-window.6 = s32[32,8,128]{2,1,0:T(8,128)S(1)} reduce-window(s32[32,8,128]{2,1,0:T(8,128)S(1)} %fusion.25, s32[]{:T(128)} %constant.66.clone.1), window={size=1x1x128 pad=0_0x0_0x127_0}, to_apply=%region_0.1 | reduce-window | flops 4161536 | bytes 262148 | tf_op jit(solution)/shard_map/reduce-window
  20.4 4.3 %scatter_custom_fusion = s32[512]{0:T(512)S(1)} fusion(s32[1024]{0:T(1024)S(1)} %bitcast.94, s32[1024]{0:T(1024)S(1)} %iota.11, s32[]{:T(128)} %constant.65.clone.1), kind=kCustom, calls=%fused_computation.100 | custom fusion | bytes 2052 | tf_op jit(solution)/shard_map/scatter | solution.py:74
  24.8 2.3 gather_fusion
  27.3 60.1 %all-gather.2.cloned.1.call-done = bf16[2,128,2048]{2,1,0:T(8,128)(2,1)} async-done(((bf16[2,128,128]{2,1,0:T(8,128)(2,1)}), bf16[2,128,2048]{2,1,0:T(8,128)(2,1)}) %all-gather.2.cloned.1.call-update) | async-done | bytes 1048592 | tf_op jit(solution)/shard_map/all_gather | solution.py:50
  87.3 1.3 slice_bitcast_fusion.1
  88.6 3.3 %gather_fusion.2 = bf16[512,2048]{1,0:T(8,128)(2,1)} fusion(bf16[128,2048]{1,0:T(8,128)(2,1)S(1)} %get-tuple-element.19, s32[1024]{0:T(1024)S(1)} %pad_clamp_fusion), kind=kCustom, calls=%fused_computation.2 | custom fusion | bytes 4196352 | tf_op jit(solution)/shard_map/gather | solution.py:80
  92.0 3.3 %gather_fusion.1 = bf16[512,2048]{1,0:T(8,128)(2,1)} fusion(bf16[128,2048]{1,0:T(8,128)(2,1)S(1)} %get-tuple-element.18, s32[1024]{0:T(1024)S(1)} %pad_clamp_fusion), kind=kCustom, calls=%fused_computation.1 | custom fusion | bytes 4196352 | tf_op jit(solution)/shard_map/gather | solution.py:81
  95.3 1.9 broadcast_select_fusion
  98.5 55.4 %all_to_all.10 = bf16[32,32,2048]{2,1,0:T(8,128)(2,1)S(1)} all-to-all(bf16[32,32,2048]{2,1,0:T(8,128)(2,1)S(1)} %pad_maximum_fusion), channel_id=1, replica_groups=mesh['dp'=32,'expert'=16] {'dp'}, dimensions={0} | all-to-all | bytes 8388608 | tf_op jit(solution)/shard_map/all_to_all | solution.py:88
  155.0 0.9 fusion.7
  155.9 0.8 copy-done.7
  156.7 0.8 fusion.15
  157.6 1.0 multiply_convert_fusion.2
  158.6 0.7 convolution_convert_fusion
  159.3 0.8 fusion.13
  160.1 0.8 add_convert_fusion
  161.4 54.4 %all_to_all.11 = bf16[32,32,2048]{2,1,0:T(8,128)(2,1)S(1)} all-to-all(bf16[32,32,2048]{2,1,0:T(8,128)(2,1)S(1)} %pad_maximum_fusion.1), channel_id=1, replica_groups=mesh['dp'=32,'expert'=16] {'dp'}, dimensions={0} | all-to-all | bytes 8388608 | tf_op jit(solution)/shard_map/all_to_all | solution.py:94
  215.8 2.5 slice_convert_fusion
  218.4 2.3 bitcast_multiply_fusion
  220.7 9.4 %scatter_custom_fusion.1 = f32[128,2048]{1,0:T(8,128)} fusion(s32[512]{0:T(512)S(1)} %get-tuple-element.26, f32[512,2048]{1,0:T(8,128)} %bitcast_multiply_fusion, f32[]{:T(128)} %constant.64.clone.1), kind=kCustom, calls=%fused_computation.40 | custom fusion | flops 1048576 | bytes 1049088 | tf_op jit(solution)/shard_map/scatter-add | solution.py:112
  230.2 9.1 %scatter_custom_fusion.2 = f32[128,2048]{1,0:T(8,128)} fusion(s32[512]{0:T(512)S(1)} %get-tuple-element.26, bf16[512,2048]{1,0:T(8,128)(2,1)} %bitcast.82, f32[]{:T(128)} %constant.64.clone.1), kind=kCustom, calls=%fused_computation.13 | custom fusion | flops 2097152 | bytes 3145732 | tf_op jit(solution)/shard_map/scatter-add | solution.py:114
  239.3 3.1 pad_maximum_fusion.2
  242.4 3.2 %fusion.6 = bf16[1,192,2048]{2,1,0:T(8,128)(2,1)} fusion(bf16[512,192]{0,1:T(8,128)(2,1)S(1)} %get-tuple-element.20, bf16[512,2048]{1,0:T(8,128)(2,1)} %bitcast.85), kind=kOutput, calls=%fused_computation.23 | convolution fusion | flops 403046400 | bytes 3080192 | tf_op jit(solution)/shard_map/dot_general | solution.py:23
  245.6 1.5 fusion.4
  247.1 1.5 fusion.5
  249.3 3.5 %scatter_custom_fusion.3 = f32[1024]{0:T(1024)S(1)} fusion(s32[512]{0:T(512)S(1)} %get-tuple-element.25, f32[512]{0:T(512)S(1)} %reshape.295, f32[]{:T(128)} %constant.64.clone.1), kind=kCustom, calls=%fused_computation.94 | custom fusion | flops 512 | bytes 4100 | tf_op jit(solution)/shard_map/scatter-add | solution.py:119
  252.8 54.7 %psum.7 = f32[128,8]{1,0:T(8,128)S(1)} all-reduce(f32[128,8]{1,0:T(8,128)S(1)} %reshape.239), channel_id=1, replica_groups=mesh['dp'=32,'expert'=16] {'expert'}, use_global_device_ids=true, to_apply=%region_9.10 | all-reduce | flops 1024 | bytes 8192 | tf_op jit(solution)/shard_map/psum | solution.py:125
  308.2 2.8 reduce-scatter.2.cloned.1.call-done
  311.0 0.9 convert.7
  (55 shorter events, 6.4 us)
Async XLA Ops:
  7.2 150.4 %copy-start = (bf16[1,192,2048]{2,1,0:T(8,128)(2,1)S(1)}, bf16[1,192,2048]{2,1,0:T(8,128)(2,1)}, u32[]{:S(2)}) copy-start(bf16[1,192,2048]{2,1,0:T(8,128)(2,1)} %param.12) | copy-start | bytes 2359300
  7.2 80.2 %all-gather.2.cloned.1.call-start = ((), (), s32[]{:S(2)}) async-start(), calls=%async_computation.3 | async-start | bytes 1114112 | tf_op jit(solution)/shard_map/all_gather | solution.py:50
  8.7 302.3 %reduce-scatter.2.cloned.1.call-start = ((), (), s32[]{:S(2)}) async-start(), calls=%async_computation.4 | async-start | bytes 2228224 | tf_op jit(solution)/shard_map/reduce_scatter | solution.py:122
  95.2 2.2 copy-start.3
  153.8 1.1 copy-start.8
  154.4 1.4 copy-start.6
  154.4 3.1 copy-start.4
  155.0 1.7 copy-start.7
  215.8 2.6 copy-start.1
  242.4 3.2 %copy-start.5 = (bf16[32,16,2048]{2,1,0:T(8,128)(2,1)S(1)}, bf16[32,16,2048]{2,1,0:T(8,128)(2,1)}, u32[]{:S(2)}) copy-start(bf16[32,16,2048]{2,1,0:T(8,128)(2,1)} %copy-done.4) | copy-start | bytes 6291460
  245.6 2.9 copy-start.2
Sparse Core Ops, SparseCore 0:
  10.6 76.7 all-gather.1
  242.5 68.4 reduce-scatter.1
where the time goes:
time: 320 us; the launch traced here: 319 us
  blocking collectives  164 us (51%)
  waiting for transfers between devices  62.9 us (20%)
  other arithmetic  45.8 us (14%)
  local copies, waits for them, and re-layouts  20.7 us (6%)
  between operations  14.4 us (4%)
  matrix products  11.1 us (3%)
    all_gather x1, waiting for transfers between devices, per_device(): lax.all_gather(jnp.stack([tokens, cotangent]), 'expert', axis=2, tiled=True)  60.1 us
    all_to_all x1, blocking collectives, per_device(): lax.all_to_all(jnp.concatenate([send_x, send_do], axis=1), 'dp', split_ax...  55.4 us
    psum x1, blocking collectives, per_device(): grad_gates = lax.psum(gate_part, 'expert')  54.7 us
    all_to_all x1, blocking collectives, per_device(): lax.all_to_all(jnp.concatenate([part_out.reshape(dp_count, capacity, feat...  54.4 us
    another operation x3, other arithmetic  9.96 us
    scatter-add x1, other arithmetic, per_device(): out_part = jnp.zeros((tok_count, features), jnp.float32).at[slot_token].a...  9.44 us
    scatter-add x1, other arithmetic, per_device(): jnp.zeros((tok_count, features), jnp.float32).at[slot_token].add(grad_float)  9.14 us
  transfers between devices with their start and end apart: 2, of which 2 were waited for; matrix products, arithmetic and copies ran while one was open for 9% of the time, Pallas kernels for 0%

commit v1 on v0

--- a/solution.py
+++ b/solution.py
@@ -47,7 +47,12 @@
 
 
 def per_device(tokens, cotangent, expert_ids, gate_weights, w_gate, w_up, w_down):
-    both = lax.all_gather(jnp.stack([tokens, cotangent]), "expert", axis=2, tiled=True)
+    both = jnp.concatenate(
+        lax.all_to_all(
+            jnp.stack([jnp.stack([tokens, cotangent])] * lax.axis_size("expert")), "expert", 0, 0
+        ),
+        axis=2,
+    )
     full_x, full_dy = (both[0], both[1])
     dp_count = lax.axis_size("dp")
     column_count = lax.axis_size("expert")

time: 320 us -> 309 us (0.966)
  the two profiles are of different devices: /device:TPU:2 before, /device:TPU:8 now
where the time goes in v1:
time: 309 us; the launch traced here: 308 us
  blocking collectives  169 us (55%)
  other arithmetic  45.2 us (15%)
  waiting for transfers between devices  32.8 us (11%)
  local copies, waits for them, and re-layouts  20.3 us (7%)
  starting transfers between devices  15.2 us (5%)
  between operations  14.4 us (5%)
  matrix products  11.1 us (4%)
    psum x1, blocking collectives, per_device(): grad_gates = lax.psum(gate_part, 'expert')  58.1 us
    all_to_all x1, blocking collectives, per_device(): lax.all_to_all(jnp.concatenate([send_x, send_do], axis=1), 'dp', split_ax...  56.6 us
    all_to_all x1, blocking collectives, per_device(): lax.all_to_all(jnp.concatenate([part_out.reshape(dp_count, capacity, feat...  54.4 us
    all_to_all x1, waiting for transfers between devices, per_device(): lax.all_to_all(jnp.stack([jnp.stack([tokens, cotangent])] * lax.axis_size...  32.8 us
    all_to_all x1, starting transfers between devices, per_device(): lax.all_to_all(jnp.stack([jnp.stack([tokens, cotangent])] * lax.axis_size...  15.2 us
    another operation x3, other arithmetic  9.96 us
    scatter-add x1, other arithmetic, per_device(): out_part = jnp.zeros((tok_count, features), jnp.float32).at[slot_token].a...  9.44 us
    scatter-add x1, other arithmetic, per_device(): jnp.zeros((tok_count, features), jnp.float32).at[slot_token].add(grad_float)  9.14 us
  transfers between devices with their start and end apart: 2, of which 1 were waited for; matrix products, arithmetic and copies ran while one was open for 9% of the time, Pallas kernels for 0%

profile of v1, /device:TPU:8, one launch (start us, length us, event | category | flops | bytes accessed | tf_op | source)
XLA Modules:
  0.0 308.2 jit_solution(9042202176892552777)
XLA Ops:
  7.2 0.9 pad_maximum_fusion.3
  8.1 1.2 stack.17
  9.3 15.2 %all-to-all-start = ((bf16[16,2,128,128]{3,2,1,0:T(8,128)(2,1)}), bf16[16,2,128,128]{3,2,1,0:T(8,128)(2,1)S(1)}, u32[]{:S(2)}, u32[]{:S(2)}) async-start(bf16[16,2,128,128]{3,2,1,0:T(8,128)(2,1)} %stack.17), calls=%async_computation | async-start | bytes 2097152 | tf_op jit(solution)/shard_map/all_to_all | solution.py:51
  25.2 9.0 %reduce-window.6 = s32[32,8,128]{2,1,0:T(8,128)S(1)} reduce-window(s32[32,8,128]{2,1,0:T(8,128)S(1)} %fusion.25, s32[]{:T(128)} %constant.66.clone.1), window={size=1x1x128 pad=0_0x0_0x127_0}, to_apply=%region_0.1 | reduce-window | flops 4161536 | bytes 262148 | tf_op jit(solution)/shard_map/reduce-window
  34.8 4.3 %scatter_custom_fusion = s32[512]{0:T(512)S(1)} fusion(s32[1024]{0:T(1024)S(1)} %bitcast.106, s32[1024]{0:T(1024)S(1)} %iota.11, s32[]{:T(128)} %constant.65.clone.1), kind=kCustom, calls=%fused_computation.100 | custom fusion | bytes 2052 | tf_op jit(solution)/shard_map/scatter | solution.py:79
  39.2 2.3 gather_fusion
  41.7 32.8 %all-to-all-done = bf16[16,2,128,128]{3,2,1,0:T(8,128)(2,1)S(1)} async-done(((bf16[16,2,128,128]{3,2,1,0:T(8,128)(2,1)}), bf16[16,2,128,128]{3,2,1,0:T(8,128)(2,1)S(1)}, u32[]{:S(2)}, u32[]{:S(2)}) %all-to-all-start) | async-done | bytes 1048608 | tf_op jit(solution)/shard_map/all_to_all | solution.py:51
  75.6 3.3 %gather_fusion.2 = bf16[512,2048]{1,0:T(8,128)(2,1)} fusion(bf16[128,2048]{1,0:T(8,128)(2,1)S(1)} %bitcast.84, s32[1024]{0:T(1024)S(1)} %pad_clamp_fusion), kind=kCustom, calls=%fused_computation.2 | custom fusion | bytes 4196352 | tf_op jit(solution)/shard_map/gather | solution.py:85
  78.9 3.3 %gather_fusion.1 = bf16[512,2048]{1,0:T(8,128)(2,1)} fusion(bf16[128,2048]{1,0:T(8,128)(2,1)S(1)} %bitcast.83, s32[1024]{0:T(1024)S(1)} %pad_clamp_fusion), kind=kCustom, calls=%fused_computation.1 | custom fusion | bytes 4196352 | tf_op jit(solution)/shard_map/gather | solution.py:86
  82.2 1.9 broadcast_select_fusion
  85.4 56.6 %all_to_all.15 = bf16[32,32,2048]{2,1,0:T(8,128)(2,1)S(1)} all-to-all(bf16[32,32,2048]{2,1,0:T(8,128)(2,1)S(1)} %pad_maximum_fusion), channel_id=1, replica_groups=mesh['dp'=32,'expert'=16] {'dp'}, dimensions={0} | all-to-all | bytes 8388608 | tf_op jit(solution)/shard_map/all_to_all | solution.py:93
  143.1 0.9 fusion.7
  144.0 0.8 copy-done.7
  144.9 0.8 fusion.15
  145.7 1.0 multiply_convert_fusion.2
  146.7 0.7 convolution_convert_fusion
  147.5 0.8 fusion.13
  148.2 0.8 add_convert_fusion
  149.6 54.4 %all_to_all.16 = bf16[32,32,2048]{2,1,0:T(8,128)(2,1)S(1)} all-to-all(bf16[32,32,2048]{2,1,0:T(8,128)(2,1)S(1)} %pad_maximum_fusion.1), channel_id=1, replica_groups=mesh['dp'=32,'expert'=16] {'dp'}, dimensions={0} | all-to-all | bytes 8388608 | tf_op jit(solution)/shard_map/all_to_all | solution.py:99
  204.0 2.5 slice_convert_fusion
  206.6 2.3 bitcast_multiply_fusion
  208.9 9.4 %scatter_custom_fusion.1 = f32[128,2048]{1,0:T(8,128)} fusion(s32[512]{0:T(512)S(1)} %get-tuple-element.32, f32[512,2048]{1,0:T(8,128)} %bitcast_multiply_fusion, f32[]{:T(128)} %constant.64.clone.1), kind=kCustom, calls=%fused_computation.40 | custom fusion | flops 1048576 | bytes 1049088 | tf_op jit(solution)/shard_map/scatter-add | solution.py:117
  218.3 9.1 %scatter_custom_fusion.2 = f32[128,2048]{1,0:T(8,128)} fusion(s32[512]{0:T(512)S(1)} %get-tuple-element.32, bf16[512,2048]{1,0:T(8,128)(2,1)} %bitcast.91, f32[]{:T(128)} %constant.64.clone.1), kind=kCustom, calls=%fused_computation.13 | custom fusion | flops 2097152 | bytes 3145732 | tf_op jit(solution)/shard_map/scatter-add | solution.py:119
  227.5 3.1 %pad_maximum_fusion.2 = f32[2,128,2048]{2,1,0:T(8,128)} fusion(f32[1,128,2048]{2,1,0:T(8,128)} %bitcast.98, f32[1,128,2048]{2,1,0:T(8,128)} %bitcast.97), kind=kLoop, calls=%fused_computation.25 | loop fusion | flops 524288 | bytes 4194304 | tf_op jit(solution)/shard_map/stack | solution.py:128
  230.6 3.2 %fusion.6 = bf16[1,192,2048]{2,1,0:T(8,128)(2,1)} fusion(bf16[512,192]{0,1:T(8,128)(2,1)S(1)} %get-tuple-element.26, bf16[512,2048]{1,0:T(8,128)(2,1)} %bitcast.94), kind=kOutput, calls=%fused_computation.23 | convolution fusion | flops 403046400 | bytes 3080192 | tf_op jit(solution)/shard_map/dot_general | solution.py:23
  233.8 1.5 fusion.4
  235.3 1.5 fusion.5
  236.7 0.6 fusion.1
  237.4 3.5 %scatter_custom_fusion.3 = f32[1024]{0:T(1024)S(1)} fusion(s32[512]{0:T(512)S(1)} %get-tuple-element.31, f32[512]{0:T(512)S(1)} %reshape.306, f32[]{:T(128)} %constant.64.clone.1), kind=kCustom, calls=%fused_computation.94 | custom fusion | flops 512 | bytes 4100 | tf_op jit(solution)/shard_map/scatter-add | solution.py:124
  241.0 58.1 %psum.7 = f32[128,8]{1,0:T(8,128)S(1)} all-reduce(f32[128,8]{1,0:T(8,128)S(1)} %reshape.250), channel_id=1, replica_groups=mesh['dp'=32,'expert'=16] {'expert'}, use_global_device_ids=true, to_apply=%region_9.10 | all-reduce | flops 1024 | bytes 8192 | tf_op jit(solution)/shard_map/psum | solution.py:130
  299.1 0.7 copy.28
  299.8 0.9 convert.7
  (63 shorter events, 6.3 us)
Async XLA Ops:
  7.2 138.6 %copy-start = (bf16[1,192,2048]{2,1,0:T(8,128)(2,1)S(1)}, bf16[1,192,2048]{2,1,0:T(8,128)(2,1)}, u32[]{:S(2)}) copy-start(bf16[1,192,2048]{2,1,0:T(8,128)(2,1)} %param.12) | copy-start | bytes 2359300
  7.2 17.4 %copy-start.9 = (s32[128,8]{0,1:T(8,128)S(1)}, s32[128,8]{0,1:T(8,128)}, u32[]{:S(2)}) copy-start(s32[128,8]{0,1:T(8,128)} %param.9) | copy-start | bytes 12292
  7.2 17.7 %copy-start.10 = (f32[128,8]{0,1:T(8,128)S(1)}, f32[128,8]{0,1:T(8,128)}, u32[]{:S(2)}) copy-start(f32[128,8]{0,1:T(8,128)} %param.10) | copy-start | bytes 12292
  9.3 65.2 %all-to-all-start = ((bf16[16,2,128,128]{3,2,1,0:T(8,128)(2,1)}), bf16[16,2,128,128]{3,2,1,0:T(8,128)(2,1)S(1)}, u32[]{:S(2)}, u32[]{:S(2)}) async-start(bf16[16,2,128,128]{3,2,1,0:T(8,128)(2,1)} %stack.17), calls=%async_computation | async-start | bytes 2097152 | tf_op jit(solution)/shard_map/all_to_all | solution.py:51
  24.5 275.3 %reduce-scatter.2.cloned.1.call-start = ((), (), s32[]{:S(2)}) async-start(), calls=%async_computation.4 | async-start | bytes 2228224 | tf_op jit(solution)/shard_map/reduce_scatter | solution.py:127
  82.2 2.2 copy-start.3
  142.0 1.1 copy-start.8
  142.6 1.4 copy-start.6
  142.6 3.1 %copy-start.4 = (bf16[32,16,2048]{2,1,0:T(8,128)(2,1)}, bf16[32,16,2048]{2,1,0:T(8,128)(2,1)S(1)}, u32[]{:S(2)}) copy-start(bf16[32,16,2048]{2,1,0:T(8,128)(2,1)S(1)} %get-tuple-element.23) | copy-start | bytes 6291460
  143.1 1.7 copy-start.7
  204.0 2.6 copy-start.1
  230.6 3.2 %copy-start.5 = (bf16[32,16,2048]{2,1,0:T(8,128)(2,1)S(1)}, bf16[32,16,2048]{2,1,0:T(8,128)(2,1)}, u32[]{:S(2)}) copy-start(bf16[32,16,2048]{2,1,0:T(8,128)(2,1)} %copy-done.4) | copy-start | bytes 6291460
  233.8 2.9 copy-start.2
Sparse Core Ops, SparseCore 0:
  230.7 68.2 reduce-scatter.1
